TPU v7x, 32 devices: a whole 2x2x4 slice. The times are simulated.
32 devices in a mesh: parts: 2 (over y), pair: 4 (over x, core), sub: 4 (over z).
Axes of the slice: x: 2, y: 2, z: 4, core: 2. Of those that a mesh axis runs over, the one named last changes fastest.
Arguments:
- features: bfloat16 [64, 1024, 256], P(('parts', 'pair'), 'sub'), parts along dimension 0, may hold values from -7 to 7
- counts: int32 [64], P('parts'), parts along dimension 0, may hold values from 256 to 1024
- pair_table: int32 [8, 4, 2], P('parts'), parts along dimension 0, may hold values from -1 to 31, as said below
- w_qk: bfloat16 [256, 256], replicated, may hold values from -0.75 to 0.75
- w_value: bfloat16 [256, 256], replicated, may hold values from -0.375 to 0.375
- w_out: bfloat16 [256, 256], replicated, may hold values from -1.5 to 1.5
- w_merge_in: bfloat16 [512, 512], replicated, may hold values from -0.25 to 0.25
- w_merge_out: bfloat16 [512, 256], replicated, may hold values from -0.25 to 0.25
Outputs:
- updated: bfloat16 [64, 1024, 256], P(('parts', 'pair'), 'sub'), parts along dimension 0
There are 2 independent parts, one for each index of `parts`. A program takes and returns all parts, laid end to end along the dimension named above; an argument that names none is the same for every part. Nothing has to cross between parts.
Inputs may be any that keep to these rules, and one draw needn't show every extreme that they name: `pair_table`: row g lists the pairs owned by index g of pair, one slot per index of sub; -1 in both entries marks an empty slot. A live slot names two images of different groups, image i belonging to group i // 8. Over the live slots of one owner, at most 2 named images (counted with repetition) belong to any one group; some owner has all 4 slots live and reaches that bound for every group.
All inputs are finite; a program needn't handle non-finite values.
Results may differ from a plain program's by a relative error of at most 0.0067.
Values may be sent and summed in bfloat16 or wider, within the bound.
A program may use at most 64 MiB of HBM per device.

v0:
```python
import jax
import jax.numpy as jnp
from jax import lax
from jax.sharding import PartitionSpec as P

HEADS = 4
ln_eps = 1e-05


def layer_norm(hidden):
    center = jnp.mean(hidden, axis=-1, keepdims=True)
    centered = hidden - center
    variance = jnp.mean(centered * centered, axis=-1, keepdims=True)
    return centered * lax.rsqrt(variance + ln_eps)


def pair_messages(left_feats, right_feats, left_count, right_count, w_qk, w_value, head_count):
    points = left_feats.shape[0]
    model_width = left_feats.shape[1]
    head_dim = model_width // head_count
    stacked = jnp.concatenate([left_feats, right_feats], axis=0)
    query_key = jnp.dot(stacked, w_qk, preferred_element_type=jnp.float32).astype(jnp.bfloat16)
    values = jnp.dot(stacked, w_value, preferred_element_type=jnp.float32).astype(jnp.bfloat16)
    row_ids = lax.broadcasted_iota(jnp.int32, (points, 1), 0)
    col_ids = lax.broadcasted_iota(jnp.int32, (1, points), 1)
    col_valid = col_ids < right_count
    row_valid = row_ids < left_count
    score_scale = head_dim ** (-0.5)
    to_left = []
    to_right = []
    for head_index in range(head_count):
        head_lo = head_index * head_dim
        q_left = query_key[:points, head_lo : head_lo + head_dim]
        q_right = query_key[points:, head_lo : head_lo + head_dim]
        v_left = values[:points, head_lo : head_lo + head_dim]
        v_right = values[points:, head_lo : head_lo + head_dim]
        scores = (
            lax.dot_general(
                q_left, q_right, (((1,), (1,)), ((), ())), preferred_element_type=jnp.float32
            )
            * score_scale
        )
        masked = jnp.where(col_valid, scores, -jnp.inf)
        row_top = jnp.max(masked, axis=1, keepdims=True)
        row_exp = jnp.exp(masked - row_top)
        row_total = jnp.sum(row_exp, axis=1, keepdims=True)
        to_left.append(
            jnp.dot(row_exp.astype(jnp.bfloat16), v_right, preferred_element_type=jnp.float32)
            / row_total
        )
        col_masked = jnp.where(row_valid, scores, -jnp.inf)
        col_top = jnp.max(col_masked, axis=0, keepdims=True)
        col_exp = jnp.exp(col_masked - col_top)
        col_total = jnp.sum(col_exp, axis=0, keepdims=True)
        summed = lax.dot_general(
            col_exp.astype(jnp.bfloat16),
            v_left,
            (((0,), (0,)), ((), ())),
            preferred_element_type=jnp.float32,
        )
        to_right.append(summed / col_total.reshape(points, 1))
    return (
        jnp.concatenate(to_left, axis=1).astype(jnp.bfloat16),
        jnp.concatenate(to_right, axis=1).astype(jnp.bfloat16),
    )


def local(features, counts, pair_table, w_qk, w_value, w_out, w_merge_in, w_merge_out):
    n_pair = lax.axis_size("pair")
    n_sub = lax.axis_size("sub")
    me_group = lax.axis_index("pair")
    me_sub = lax.axis_index("sub")
    img_grp, kp_block, model_width = features.shape
    per_src = 2 * n_sub // n_pair
    positions = 2 * n_sub
    slot_table = pair_table.reshape(n_pair, positions)
    slot_live = slot_table >= 0
    source = jnp.where(slot_live, slot_table // img_grp, -1)
    group_ids = jnp.arange(n_pair, dtype=jnp.int32)
    src_hot = (source[:, :, None] == group_ids[None, None, :]).astype(jnp.int32)
    src_rank = jnp.sum((jnp.cumsum(src_hot, axis=1) - 1) * src_hot, axis=2)
    src_rank = jnp.where(slot_live, src_rank, -1)
    slot_ids = jnp.arange(per_src, dtype=jnp.int32)
    from_me = source == me_group
    send_match = from_me[:, None, :] & (src_rank[:, None, :] == slot_ids[None, :, None])
    send_local = jnp.sum(
        jnp.where(send_match, slot_table[:, None, :] - me_group * img_grp, 0), axis=2
    )
    send_ok = jnp.any(send_match, axis=2)
    my_table = lax.dynamic_index_in_dim(slot_table, me_group, 0, keepdims=False)
    my_live = lax.dynamic_index_in_dim(slot_live, me_group, 0, keepdims=False)
    my_source = lax.dynamic_index_in_dim(source, me_group, 0, keepdims=False)
    my_rank = lax.dynamic_index_in_dim(src_rank, me_group, 0, keepdims=False)
    outgoing = jnp.take(features, send_local.reshape(-1), axis=0).reshape(
        n_pair, per_src, kp_block, model_width
    )
    outgoing = jnp.where(send_ok[:, :, None, None], outgoing, jnp.zeros_like(outgoing))
    arrived = lax.all_to_all(outgoing, "pair", split_axis=0, concat_axis=0, tiled=True)
    flat_index = jnp.maximum(my_source * per_src + my_rank, 0)
    picked = jnp.take(arrived.reshape(n_pair * per_src, kp_block, model_width), flat_index, axis=0)
    picked = jnp.where(my_live[:, None, None], picked, jnp.zeros_like(picked))
    grouped = picked.reshape(n_sub, 2, kp_block, model_width)
    pair_rows = lax.all_to_all(grouped, "sub", split_axis=0, concat_axis=2, tiled=True)
    slot_pair = jnp.maximum(lax.dynamic_slice_in_dim(my_table, 2 * me_sub, 2), 0)
    pair_counts = jnp.take(counts, slot_pair)
    to_left, to_right = pair_messages(
        pair_rows[0, 0], pair_rows[0, 1], pair_counts[0], pair_counts[1], w_qk, w_value, HEADS
    )
    outbound = jnp.stack([to_left, to_right], axis=0)[None]
    returned = lax.all_to_all(outbound, "sub", split_axis=2, concat_axis=0, tiled=True)
    returned = returned.reshape(positions, kp_block, model_width)
    returned = jnp.where(my_live[:, None, None], returned, jnp.zeros_like(returned))
    position_ids = jnp.arange(positions, dtype=jnp.int32)
    inverse = (
        (my_source[None, None, :] == group_ids[:, None, None])
        & (my_rank[None, None, :] == slot_ids[None, :, None])
        & my_live[None, None, :]
    )
    inv_pos = jnp.sum(jnp.where(inverse, position_ids[None, None, :], 0), axis=2)
    inv_ok = jnp.any(inverse, axis=2)
    homeward = jnp.take(returned, inv_pos.reshape(-1), axis=0).reshape(
        n_pair, per_src, kp_block, model_width
    )
    homeward = jnp.where(inv_ok[:, :, None, None], homeward, jnp.zeros_like(homeward))
    home_msgs = lax.all_to_all(homeward, "pair", split_axis=0, concat_axis=0, tiled=True)
    local_ids = jnp.arange(img_grp, dtype=jnp.int32)
    owner_hot = ((send_local.reshape(1, -1) == local_ids[:, None]) & send_ok.reshape(1, -1)).astype(
        jnp.bfloat16
    )
    msg_total = jnp.dot(
        owner_hot,
        home_msgs.reshape(n_pair * per_src, kp_block * model_width),
        preferred_element_type=jnp.float32,
    )
    global_ids = me_group * img_grp + local_ids
    use_count = jnp.sum(
        (pair_table.reshape(1, -1) == global_ids[:, None]).astype(jnp.int32), axis=1
    )
    divisor = jnp.maximum(use_count, 1).astype(jnp.float32)
    mean_msg = (msg_total / divisor[:, None]).astype(jnp.bfloat16)
    own_rows = features.reshape(-1, model_width)
    lifted = jnp.dot(
        mean_msg.reshape(-1, model_width), w_out, preferred_element_type=jnp.float32
    ).astype(jnp.bfloat16)
    hidden = jnp.dot(own_rows, w_merge_in[:model_width], preferred_element_type=jnp.float32)
    hidden = hidden + jnp.dot(lifted, w_merge_in[model_width:], preferred_element_type=jnp.float32)
    active = jax.nn.gelu(layer_norm(hidden), approximate=False).astype(jnp.bfloat16)
    updated = own_rows.astype(jnp.float32) + jnp.dot(
        active, w_merge_out, preferred_element_type=jnp.float32
    )
    return updated.astype(jnp.bfloat16).reshape(img_grp, kp_block, model_width)


def solution(mesh):
    in_specs = (
        P(("parts", "pair"), "sub", None),
        P("parts"),
        P("parts", None, None),
        P(),
        P(),
        P(),
        P(),
        P(),
    )
    out_specs = P(("parts", "pair"), "sub", None)
    return jax.shard_map(local, mesh=mesh, in_specs=in_specs, out_specs=out_specs, check_vma=False)
```

profile of v0, /device:TPU:0, one launch (start us, length us, event | category | flops | bytes accessed | tf_op | source)
XLA Modules:
  0.0 154.1 jit_solution(910745184698559716)
XLA Ops:
  0.0 0.8 copy.48
  1.0 0.7 reduce_window_sum.11
  2.8 1.8 %gather_fusion.1 = bf16[8,256,256]{2,1,0:T(8,128)(2,1)S(1)} fusion(bf16[8,256,256]{2,1,0:T(8,128)(2,1)} %param.10, s32[1024]{0:T(1024)S(1)} %pad_clamp_fusion.2), kind=kCustom, calls=%fused_computation.clone | custom fusion | bytes 2097184 | tf_op jit(solution)/shard_map/jit(_take)/gather | solution.py:94
  4.6 0.2 broadcast_select_fusion.1
  4.8 1.1 broadcast_select_fusion.2
  5.9 4.4 %all-to-all-start = ((bf16[4,2,256,256]{3,2,1,0:T(8,128)(2,1)}), bf16[4,2,256,256]{3,2,1,0:T(8,128)(2,1)S(1)}, u32[]{:S(2)}, u32[]{:S(2)}) async-start(bf16[4,2,256,256]{3,2,1,0:T(8,128)(2,1)} %broadcast_select_fusion.2), calls=%async_computation | async-start | bytes 2097152 | tf_op jit(solution)/shard_map/all_to_all | solution.py:98
  10.3 14.4 %all-to-all-done = bf16[4,2,256,256]{3,2,1,0:T(8,128)(2,1)S(1)} async-done(((bf16[4,2,256,256]{3,2,1,0:T(8,128)(2,1)}), bf16[4,2,256,256]{3,2,1,0:T(8,128)(2,1)S(1)}, u32[]{:S(2)}, u32[]{:S(2)}) %all-to-all-start) | async-done | bytes 1048608 | tf_op jit(solution)/shard_map/all_to_all | solution.py:98
  24.7 0.6 gather_fusion.2
  25.4 1.2 select_select_fusion
  26.5 5.6 %all-to-all-start.1 = ((bf16[4,2,256,256]{3,2,1,0:T(8,128)(2,1)}), bf16[4,2,256,256]{3,2,1,0:T(8,128)(2,1)S(1)}, u32[]{:S(2)}, u32[]{:S(2)}) async-start(bf16[4,2,256,256]{3,2,1,0:T(8,128)(2,1)} %bitcast.8), calls=%async_computation.1 | async-start | bytes 2097152 | tf_op jit(solution)/shard_map/all_to_all | solution.py:103
  32.1 0.2 fusion.161
  32.3 0.6 gather_fusion
  33.0 0.2 compare_reduce_fusion
  33.2 0.6 fusion.213
  33.8 1.3 iota_compare_fusion.1
  35.0 22.5 %all-to-all-done.1 = bf16[4,2,256,256]{3,2,1,0:T(8,128)(2,1)S(1)} async-done(((bf16[4,2,256,256]{3,2,1,0:T(8,128)(2,1)}), bf16[4,2,256,256]{3,2,1,0:T(8,128)(2,1)S(1)}, u32[]{:S(2)}, u32[]{:S(2)}) %all-to-all-start.1) | async-done | bytes 1048608 | tf_op jit(solution)/shard_map/all_to_all | solution.py:103
  57.7 0.5 convolution_convert_fusion.2
  58.2 0.7 fusion.141
  58.9 0.7 fusion.137
  59.7 0.7 fusion.133
  60.4 0.5 convolution_convert_fusion.1
  60.9 1.9 %select_reduce_fusion.7 = (f32[1024]{0:T(1024)S(1)}, f32[1024]{0:T(1024)S(1)}, f32[1024]{0:T(1024)S(1)}, f32[1024]{0:T(1024)S(1)}, f32[1024,1024]{1,0:T(8,128)S(1)}) fusion(pred[1024]{0:T(1024)(128)(4,1)S(1)} %get-tuple-element.47, f32[1024,1024]{1,0:T(8,128)S(1)} %fusion.141, f32[1024,1024]{1,0:T(8,128)S(1)} %fusion.137, f32[1024,1024]{1,0:T(8,128)S(1)} %fusion.133, ...), kind=kOutput, calls=%fused_computation.41 | convolution fusion | flops 146796544 | bytes 17056768 | tf_op jit(solution)/shard_map/dot_general | solution.py:38
  62.8 6.2 %fusion.17 = (f32[1024]{0:T(1024)S(1)}, f32[1024]{0:T(1024)S(1)}, f32[1024]{0:T(1024)S(1)}, f32[1024]{0:T(1024)S(1)}, f32[1024]{0:T(1024)S(1)}, /*index=5*/f32[1024]{0:T(1024)S(1)}, f32[1024]{0:T(1024)S(1)}, f32[1024]{0:T(1024)S(1)}) fusion(f32[1024,1024]{1,0:T(8,128)S(1)} %fusion.133, f32[1024]{0:T(1024)S(1)} %get-tuple-element.23, ...), kind=kLoop, calls=%fused_computation.48 | loop fusion | flops 25157632 | bytes 16828416 | tf_op jit(solution)/shard_map/reduce_sum | solution.py:46
  69.0 4.2 %fusion.19 = (f32[1024]{0:T(1024)S(1)}, f32[1024]{0:T(1024)S(1)}, f32[1024]{0:T(1024)S(1)}, f32[1024]{0:T(1024)S(1)}) fusion(f32[1024,1024]{1,0:T(8,128)S(1)} %get-tuple-element.39, f32[1024]{0:T(1024)S(1)} %get-tuple-element.14, pred[1024]{0:T(1024)(128)(4,1)S(1)} %get-tuple-element.46, f32[1024]{0:T(1024)S(1)} %get-tuple-element.16, ...), kind=kLoop, calls=%fused_computation.50 | loop fusion | flops 16773120 | bytes 16811008 | tf_op jit(solution)/shard_map/reduce_sum | solution.py:54
  73.2 1.1 fusion.95
  74.3 1.0 fusion.59
  75.4 1.1 fusion.122
  76.5 1.0 fusion.86
  77.6 1.1 fusion.113
  78.7 1.0 fusion.77
  79.8 1.0 fusion.68
  80.8 1.1 fusion.104
  82.0 2.0 %copy.61 = bf16[1,2,1024,256]{3,1,0,2:T(2,128)(2,1)} copy(bf16[1,2,1024,256]{2,3,1,0:T(8,128)(2,1)S(1)} %maximum_bitcast_fusion) | data formatting | bytes 2097152 | tf_op jit(solution)/shard_map/broadcast_in_dim | solution.py:109
  84.1 3.5 %all-to-all-start.2 = ((bf16[1,2,1024,256]{3,1,0,2:T(2,128)(2,1)}), bf16[1,2,1024,256]{3,1,0,2:T(2,128)(2,1)S(1)}, u32[]{:S(2)}, u32[]{:S(2)}) async-start(bf16[1,2,1024,256]{3,1,0,2:T(2,128)(2,1)} %copy.61), calls=%async_computation.2 | async-start | bytes 2097152 | tf_op jit(solution)/shard_map/all_to_all | solution.py:110
  88.2 24.7 %all-to-all-done.2 = bf16[1,2,1024,256]{3,1,0,2:T(2,128)(2,1)S(1)} async-done(((bf16[1,2,1024,256]{3,1,0,2:T(2,128)(2,1)}), bf16[1,2,1024,256]{3,1,0,2:T(2,128)(2,1)S(1)}, u32[]{:S(2)}, u32[]{:S(2)}) %all-to-all-start.2) | async-done | bytes 1048608 | tf_op jit(solution)/shard_map/all_to_all | solution.py:110
  113.2 0.6 gather_fusion.3
  114.0 1.1 broadcast_select_fusion.3
  115.1 3.7 %all-to-all-start.3 = ((bf16[4,2,256,256]{3,2,1,0:T(8,128)(2,1)}), bf16[4,2,256,256]{3,2,1,0:T(8,128)(2,1)S(1)}, u32[]{:S(2)}, u32[]{:S(2)}) async-start(bf16[4,2,256,256]{3,2,1,0:T(8,128)(2,1)} %broadcast_select_fusion.3), calls=%async_computation.3 | async-start | bytes 2097152 | tf_op jit(solution)/shard_map/all_to_all | solution.py:125
  118.9 0.2 convert_reduce_fusion
  119.1 2.7 %fusion.126 = f32[2048,512]{0,1:T(8,128)} fusion(bf16[2048,256]{1,0:T(8,128)(2,1)S(1)} %bitcast.65, bf16[512,512]{1,0:T(8,128)(2,1)S(1)} %copy-done.4), kind=kOutput, calls=%fused_computation.115 | convolution fusion | flops 536870912 | bytes 5505024 | tf_op jit(solution)/shard_map/dot_general | solution.py:145
  121.8 11.3 %all-to-all-done.3 = bf16[4,2,256,256]{3,2,1,0:T(8,128)(2,1)S(1)} async-done(((bf16[4,2,256,256]{3,2,1,0:T(8,128)(2,1)}), bf16[4,2,256,256]{3,2,1,0:T(8,128)(2,1)S(1)}, u32[]{:S(2)}, u32[]{:S(2)}) %all-to-all-start.3) | async-done | bytes 1048608 | tf_op jit(solution)/shard_map/all_to_all | solution.py:125
  133.1 0.6 copy.65
  133.7 0.4 fusion
  134.1 0.5 reshape.377
  134.6 5.3 %fusion.214 = (f32[2048]{0:T(1024)S(1)}, f32[2048,512]{0,1:T(8,128)}) fusion(f32[2048,512]{0,1:T(8,128)} %fusion.126, bf16[512,512]{1,0:T(8,128)(2,1)} %param.16, bf16[2048,256]{1,0:T(8,128)(2,1)S(1)} %reshape.377, bf16[256,256]{1,0:T(8,128)(2,1)S(1)} %copy-done.5), kind=kOutput, calls=%fused_computation.240 | convolution fusion | flops 807925760 | bytes 9838592 | tf_op jit(solution)/shard_map/dot_general | solution.py:146
  139.9 2.8 %multiply_reduce_fusion = f32[2048]{0:T(1024)S(1)} fusion(f32[2048,512]{0,1:T(8,128)} %get-tuple-element.41, f32[2048]{0:T(1024)S(1)} %broadcast_multiply_fusion), kind=kLoop, calls=%fused_computation.23 | loop fusion | flops 3143680 | bytes 4210688 | tf_op jit(solution)/shard_map/reduce_sum | solution.py:13
  142.8 0.6 copy-done.2
  143.4 10.8 %fusion.27 = bf16[2048,256]{1,0:T(8,128)(2,1)} fusion(bf16[512,256]{1,0:T(8,128)(2,1)S(1)} %copy-done, bf16[2048,256]{1,0:T(8,128)(2,1)S(1)} %bitcast.66, f32[2048,512]{0,1:T(8,128)S(1)} %copy-done.2, f32[2048]{0:T(1024)S(1)} %add_rsqrt_fusion, f32[2048]{0:T(1024)S(1)} %broadcast_multiply_fusion), kind=kOutput, calls=%fused_computation.60 | convolution fusion | flops 608698368 | bytes 6569984 | tf_op jit(solution)/shard_map/dot_general | solution.py:148
  (59 shorter events, 2.6 us)
Async XLA Ops:
  0.0 142.7 %copy-start = (bf16[512,256]{1,0:T(8,128)(2,1)S(1)}, bf16[512,256]{1,0:T(8,128)(2,1)}, u32[]{:S(2)}) copy-start(bf16[512,256]{1,0:T(8,128)(2,1)} %param.17) | copy-start | bytes 786436
  5.9 26.4 %copy-start.1 = (s32[32]{0:T(128)S(1)}, s32[32]{0:T(128)}, u32[]{:S(2)}) copy-start(s32[32]{0:T(128)} %param.11) | copy-start | bytes 388
  5.9 18.8 %all-to-all-start = ((bf16[4,2,256,256]{3,2,1,0:T(8,128)(2,1)}), bf16[4,2,256,256]{3,2,1,0:T(8,128)(2,1)S(1)}, u32[]{:S(2)}, u32[]{:S(2)}) async-start(bf16[4,2,256,256]{3,2,1,0:T(8,128)(2,1)} %broadcast_select_fusion.2), calls=%async_computation | async-start | bytes 2097152 | tf_op jit(solution)/shard_map/all_to_all | solution.py:98
  25.4 32.4 %copy-start.7 = (bf16[256,256]{1,0:T(8,128)(2,1)S(1)}, bf16[256,256]{1,0:T(8,128)(2,1)}, u32[]{:S(2)}) copy-start(bf16[256,256]{1,0:T(8,128)(2,1)} %param.13) | copy-start | bytes 393220
  26.5 31.0 %all-to-all-start.1 = ((bf16[4,2,256,256]{3,2,1,0:T(8,128)(2,1)}), bf16[4,2,256,256]{3,2,1,0:T(8,128)(2,1)S(1)}, u32[]{:S(2)}, u32[]{:S(2)}) async-start(bf16[4,2,256,256]{3,2,1,0:T(8,128)(2,1)} %bitcast.8), calls=%async_computation.1 | async-start | bytes 2097152 | tf_op jit(solution)/shard_map/all_to_all | solution.py:103
  58.9 1.5 copy-start.8
  82.0 5.7 %copy-start.6 = (s32[4,4,2]{1,2,0:T(2,128)S(1)}, s32[4,4,2]{1,2,0:T(2,128)}, u32[]{:S(2)}) copy-start(s32[4,4,2]{1,2,0:T(2,128)} %param.12) | copy-start | bytes 388
  84.1 28.8 %all-to-all-start.2 = ((bf16[1,2,1024,256]{3,1,0,2:T(2,128)(2,1)}), bf16[1,2,1024,256]{3,1,0,2:T(2,128)(2,1)S(1)}, u32[]{:S(2)}, u32[]{:S(2)}) async-start(bf16[1,2,1024,256]{3,1,0,2:T(2,128)(2,1)} %copy.61), calls=%async_computation.2 | async-start | bytes 2097152 | tf_op jit(solution)/shard_map/all_to_all | solution.py:110
  113.2 5.9 %copy-start.3 = (bf16[8,256,256]{2,1,0:T(8,128)(2,1)S(1)}, bf16[8,256,256]{2,1,0:T(8,128)(2,1)}, u32[]{:S(2)}) copy-start(bf16[8,256,256]{2,1,0:T(8,128)(2,1)} %param.10) | copy-start | bytes 3145732
  113.9 5.3 %copy-start.4 = (bf16[512,512]{1,0:T(8,128)(2,1)S(1)}, bf16[512,512]{1,0:T(8,128)(2,1)}, u32[]{:S(2)}) copy-start(bf16[512,512]{1,0:T(8,128)(2,1)} %param.16) | copy-start | bytes 1572868
  115.1 17.9 %all-to-all-start.3 = ((bf16[4,2,256,256]{3,2,1,0:T(8,128)(2,1)}), bf16[4,2,256,256]{3,2,1,0:T(8,128)(2,1)S(1)}, u32[]{:S(2)}, u32[]{:S(2)}) async-start(bf16[4,2,256,256]{3,2,1,0:T(8,128)(2,1)} %broadcast_select_fusion.3), calls=%async_computation.3 | async-start | bytes 2097152 | tf_op jit(solution)/shard_map/all_to_all | solution.py:125
  133.7 0.9 copy-start.5
  139.9 3.4 %copy-start.2 = (f32[2048,512]{0,1:T(8,128)S(1)}, f32[2048,512]{0,1:T(8,128)}, u32[]{:S(2)}) copy-start(f32[2048,512]{0,1:T(8,128)} %get-tuple-element.41) | copy-start | bytes 12582916
where the time goes:
time: 155 us; the launch traced here: 154 us
  waiting for transfers between devices  72.9 us (47%)
  matrix products  33 us (21%)
  other arithmetic  20.4 us (13%)
  starting transfers between devices  17.2 us (11%)
  local copies, waits for them, and re-layouts  10.3 us (7%)
    all_to_all x1, waiting for transfers between devices, local(): lax.all_to_all(outbound, 'sub', split_axis=2, concat_axis=0, tiled=True)  24.7 us
    all_to_all x1, waiting for transfers between devices, local(): lax.all_to_all(grouped, 'sub', split_axis=0, concat_axis=2, tiled=True)  22.5 us
    all_to_all x1, waiting for transfers between devices, local(): lax.all_to_all(outgoing, 'pair', split_axis=0, concat_axis=0, tiled=True)  14.4 us
    all_to_all x1, waiting for transfers between devices, local(): lax.all_to_all(homeward, 'pair', split_axis=0, concat_axis=0, tiled=True)  11.3 us
    dot_general x1, matrix products, local(): jnp.dot(active, w_merge_out, preferred_element_type=jnp.float32)  10.8 us
    reduce_sum x1, other arithmetic, pair_messages(): row_total = jnp.sum(row_exp, axis=1, keepdims=True)  6.18 us
    all_to_all x1, starting transfers between devices, local(): lax.all_to_all(grouped, 'sub', split_axis=0, concat_axis=2, tiled=True)  5.6 us
    dot_general x1, matrix products, local(): jnp.dot(lifted, w_merge_in[model_width:], preferred_element_type=jnp.floa...  5.34 us
  transfers between devices with their start and end apart: 4, of which 4 were waited for; matrix products, arithmetic and copies ran while one was open for 4% of the time, Pallas kernels for 0%

commit v1 on v0

--- a/solution.py
+++ b/solution.py
@@ -107,7 +107,10 @@
         pair_rows[0, 0], pair_rows[0, 1], pair_counts[0], pair_counts[1], w_qk, w_value, HEADS
     )
     outbound = jnp.stack([to_left, to_right], axis=0)[None]
-    returned = lax.all_to_all(outbound, "sub", split_axis=2, concat_axis=0, tiled=True)
+    returned = jnp.concatenate(
+        lax.all_to_all(jnp.stack(jnp.split(outbound, lax.axis_size("sub"), axis=2)), "sub", 0, 0),
+        axis=0,
+    )
     returned = returned.reshape(positions, kp_block, model_width)
     returned = jnp.where(my_live[:, None, None], returned, jnp.zeros_like(returned))
     position_ids = jnp.arange(positions, dtype=jnp.int32)

time: 155 us -> 154 us (level)
  local copies, waits for them, and re-layouts: 10.3 us -> 8.64 us
    broadcast_in_dim x1 -> x0, local copies, waits for them, and re-layouts: 2.04 us -> none  [local(): outbound = jnp.stack([to_left, to_right], axis=0)[None]]
where the time goes in v1:
time: 154 us
  waiting for transfers between devices  72.9 us (47%)
  matrix products  33 us (21%)
  other arithmetic  21.5 us (14%)
  starting transfers between devices  17.2 us (11%)
  local copies, waits for them, and re-layouts  8.64 us (6%)
    all_to_all x1, waiting for transfers between devices, local(): lax.all_to_all(jnp.stack(jnp.split(outbound, lax.axis_size('sub'), axis=2...  24.7 us
    all_to_all x1, waiting for transfers between devices, local(): lax.all_to_all(grouped, 'sub', split_axis=0, concat_axis=2, tiled=True)  22.5 us
    all_to_all x1, waiting for transfers between devices, local(): lax.all_to_all(outgoing, 'pair', split_axis=0, concat_axis=0, tiled=True)  14.4 us
    all_to_all x1, waiting for transfers between devices, local(): lax.all_to_all(homeward, 'pair', split_axis=0, concat_axis=0, tiled=True)  11.3 us
    dot_general x1, matrix products, local(): jnp.dot(active, w_merge_out, preferred_element_type=jnp.float32)  10.8 us
    reduce_sum x1, other arithmetic, pair_messages(): row_total = jnp.sum(row_exp, axis=1, keepdims=True)  6.18 us
    all_to_all x1, starting transfers between devices, local(): lax.all_to_all(grouped, 'sub', split_axis=0, concat_axis=2, tiled=True)  5.6 us
    dot_general x1, matrix products, local(): jnp.dot(lifted, w_merge_in[model_width:], preferred_element_type=jnp.floa...  5.34 us
  transfers between devices with their start and end apart: 4, of which 4 were waited for; matrix products, arithmetic and copies ran while one was open for 4% of the time, Pallas kernels for 0%

profile of v1, /device:TPU:0, one launch (start us, length us, event | category | flops | bytes accessed | tf_op | source)
XLA Modules:
  0.0 153.6 jit_solution(7211658153560071123)
XLA Ops:
  0.0 0.8 copy.32
  1.0 0.7 reduce_window_sum.11
  2.8 1.8 %gather_fusion.1 = bf16[8,256,256]{2,1,0:T(8,128)(2,1)S(1)} fusion(bf16[8,256,256]{2,1,0:T(8,128)(2,1)} %param.10, s32[1024]{0:T(1024)S(1)} %pad_clamp_fusion.2), kind=kCustom, calls=%fused_computation.clone | custom fusion | bytes 2097184 | tf_op jit(solution)/shard_map/jit(_take)/gather | solution.py:94
  4.8 1.1 broadcast_select_fusion.3
  5.9 4.4 %all-to-all-start = ((bf16[4,2,256,256]{3,2,1,0:T(8,128)(2,1)}), bf16[4,2,256,256]{3,2,1,0:T(8,128)(2,1)S(1)}, u32[]{:S(2)}, u32[]{:S(2)}) async-start(bf16[4,2,256,256]{3,2,1,0:T(8,128)(2,1)} %broadcast_select_fusion.3), calls=%async_computation | async-start | bytes 2097152 | tf_op jit(solution)/shard_map/all_to_all | solution.py:98
  10.3 14.4 %all-to-all-done = bf16[4,2,256,256]{3,2,1,0:T(8,128)(2,1)S(1)} async-done(((bf16[4,2,256,256]{3,2,1,0:T(8,128)(2,1)}), bf16[4,2,256,256]{3,2,1,0:T(8,128)(2,1)S(1)}, u32[]{:S(2)}, u32[]{:S(2)}) %all-to-all-start) | async-done | bytes 1048608 | tf_op jit(solution)/shard_map/all_to_all | solution.py:98
  24.7 0.6 gather_fusion.2
  25.4 1.2 select_select_fusion
  26.5 5.6 %all-to-all-start.1 = ((bf16[4,2,256,256]{3,2,1,0:T(8,128)(2,1)}), bf16[4,2,256,256]{3,2,1,0:T(8,128)(2,1)S(1)}, u32[]{:S(2)}, u32[]{:S(2)}) async-start(bf16[4,2,256,256]{3,2,1,0:T(8,128)(2,1)} %bitcast.8), calls=%async_computation.1 | async-start | bytes 2097152 | tf_op jit(solution)/shard_map/all_to_all | solution.py:103
  32.1 0.2 fusion.161
  32.3 0.6 gather_fusion
  33.0 0.2 compare_reduce_fusion
  33.2 0.6 fusion.213
  33.8 1.3 iota_compare_fusion.1
  35.0 22.5 %all-to-all-done.1 = bf16[4,2,256,256]{3,2,1,0:T(8,128)(2,1)S(1)} async-done(((bf16[4,2,256,256]{3,2,1,0:T(8,128)(2,1)}), bf16[4,2,256,256]{3,2,1,0:T(8,128)(2,1)S(1)}, u32[]{:S(2)}, u32[]{:S(2)}) %all-to-all-start.1) | async-done | bytes 1048608 | tf_op jit(solution)/shard_map/all_to_all | solution.py:103
  57.7 0.5 convolution_convert_fusion.2
  58.2 0.7 fusion.141
  59.0 0.7 fusion.137
  59.7 0.7 fusion.133
  60.4 0.5 convolution_convert_fusion.1
  60.9 1.9 %select_reduce_fusion.7 = (f32[1024]{0:T(1024)S(1)}, f32[1024]{0:T(1024)S(1)}, f32[1024]{0:T(1024)S(1)}, f32[1024]{0:T(1024)S(1)}, f32[1024,1024]{1,0:T(8,128)S(1)}) fusion(pred[1024]{0:T(1024)(128)(4,1)S(1)} %get-tuple-element.49, f32[1024,1024]{1,0:T(8,128)S(1)} %fusion.141, f32[1024,1024]{1,0:T(8,128)S(1)} %fusion.137, f32[1024,1024]{1,0:T(8,128)S(1)} %fusion.133, ...), kind=kOutput, calls=%fused_computation.41 | convolution fusion | flops 146796544 | bytes 17056768 | tf_op jit(solution)/shard_map/dot_general | solution.py:38
  62.8 6.2 %fusion.17 = (f32[1024]{0:T(1024)S(1)}, f32[1024]{0:T(1024)S(1)}, f32[1024]{0:T(1024)S(1)}, f32[1024]{0:T(1024)S(1)}, f32[1024]{0:T(1024)S(1)}, /*index=5*/f32[1024]{0:T(1024)S(1)}, f32[1024]{0:T(1024)S(1)}, f32[1024]{0:T(1024)S(1)}) fusion(f32[1024,1024]{1,0:T(8,128)S(1)} %fusion.133, f32[1024]{0:T(1024)S(1)} %get-tuple-element.23, ...), kind=kLoop, calls=%fused_computation.48 | loop fusion | flops 25157632 | bytes 16828416 | tf_op jit(solution)/shard_map/reduce_sum | solution.py:46
  69.0 4.2 %fusion.19 = (f32[1024]{0:T(1024)S(1)}, f32[1024]{0:T(1024)S(1)}, f32[1024]{0:T(1024)S(1)}, f32[1024]{0:T(1024)S(1)}) fusion(f32[1024,1024]{1,0:T(8,128)S(1)} %get-tuple-element.43, f32[1024]{0:T(1024)S(1)} %get-tuple-element.14, pred[1024]{0:T(1024)(128)(4,1)S(1)} %get-tuple-element.48, f32[1024]{0:T(1024)S(1)} %get-tuple-element.16, ...), kind=kLoop, calls=%fused_computation.50 | loop fusion | flops 16773120 | bytes 16811008 | tf_op jit(solution)/shard_map/reduce_sum | solution.py:54
  73.2 1.1 fusion.95
  74.3 1.0 fusion.59
  75.4 1.1 fusion.122
  76.5 1.0 fusion.86
  77.6 1.1 fusion.113
  78.7 1.0 fusion.77
  79.8 1.0 fusion.68
  80.8 1.1 fusion.104
  82.1 1.1 pad_maximum_fusion.1
  83.2 3.5 %all-to-all-start.2 = ((bf16[4,1,2,256,256]{3,4,2,1,0:T(8,128)(2,1)}), bf16[4,1,2,256,256]{3,4,2,1,0:T(8,128)(2,1)S(1)}, u32[]{:S(2)}, u32[]{:S(2)}) async-start(bf16[4,1,2,256,256]{3,4,2,1,0:T(8,128)(2,1)} %pad_maximum_fusion.1), calls=%async_computation.2 | async-start | bytes 2097152 | tf_op jit(solution)/shard_map/all_to_all | solution.py:111
  87.3 24.7 %all-to-all-done.2 = bf16[4,1,2,256,256]{3,4,2,1,0:T(8,128)(2,1)S(1)} async-done(((bf16[4,1,2,256,256]{3,4,2,1,0:T(8,128)(2,1)}), bf16[4,1,2,256,256]{3,4,2,1,0:T(8,128)(2,1)S(1)}, u32[]{:S(2)}, u32[]{:S(2)}) %all-to-all-start.2) | async-done | bytes 1048608 | tf_op jit(solution)/shard_map/all_to_all | solution.py:111
  112.0 0.5 copy.45
  112.7 0.6 gather_fusion.3
  113.5 1.1 broadcast_select_fusion.4
  114.6 3.7 %all-to-all-start.3 = ((bf16[4,2,256,256]{3,2,1,0:T(8,128)(2,1)}), bf16[4,2,256,256]{3,2,1,0:T(8,128)(2,1)S(1)}, u32[]{:S(2)}, u32[]{:S(2)}) async-start(bf16[4,2,256,256]{3,2,1,0:T(8,128)(2,1)} %broadcast_select_fusion.4), calls=%async_computation.3 | async-start | bytes 2097152 | tf_op jit(solution)/shard_map/all_to_all | solution.py:128
  118.4 0.2 convert_reduce_fusion
  118.6 2.7 %fusion.126 = f32[2048,512]{0,1:T(8,128)} fusion(bf16[2048,256]{1,0:T(8,128)(2,1)S(1)} %bitcast.69, bf16[512,512]{1,0:T(8,128)(2,1)S(1)} %copy-done.4), kind=kOutput, calls=%fused_computation.120 | convolution fusion | flops 536870912 | bytes 5505024 | tf_op jit(solution)/shard_map/dot_general | solution.py:148
  121.2 11.3 %all-to-all-done.3 = bf16[4,2,256,256]{3,2,1,0:T(8,128)(2,1)S(1)} async-done(((bf16[4,2,256,256]{3,2,1,0:T(8,128)(2,1)}), bf16[4,2,256,256]{3,2,1,0:T(8,128)(2,1)S(1)}, u32[]{:S(2)}, u32[]{:S(2)}) %all-to-all-start.3) | async-done | bytes 1048608 | tf_op jit(solution)/shard_map/all_to_all | solution.py:128
  132.5 0.6 copy.47
  133.1 0.4 fusion
  133.5 0.5 reshape.372
  134.0 5.3 %fusion.214 = (f32[2048]{0:T(1024)S(1)}, f32[2048,512]{0,1:T(8,128)}) fusion(f32[2048,512]{0,1:T(8,128)} %fusion.126, bf16[512,512]{1,0:T(8,128)(2,1)} %param.16, bf16[2048,256]{1,0:T(8,128)(2,1)S(1)} %reshape.372, bf16[256,256]{1,0:T(8,128)(2,1)S(1)} %copy-done.5), kind=kOutput, calls=%fused_computation.245 | convolution fusion | flops 807925760 | bytes 9838592 | tf_op jit(solution)/shard_map/dot_general | solution.py:149
  139.4 2.8 %multiply_reduce_fusion = f32[2048]{0:T(1024)S(1)} fusion(f32[2048,512]{0,1:T(8,128)} %get-tuple-element.45, f32[2048]{0:T(1024)S(1)} %broadcast_multiply_fusion), kind=kLoop, calls=%fused_computation.23 | loop fusion | flops 3143680 | bytes 4210688 | tf_op jit(solution)/shard_map/reduce_sum | solution.py:13
  142.2 0.6 copy-done.2
  142.8 10.8 %fusion.27 = bf16[2048,256]{1,0:T(8,128)(2,1)} fusion(bf16[512,256]{1,0:T(8,128)(2,1)S(1)} %copy-done, bf16[2048,256]{1,0:T(8,128)(2,1)S(1)} %bitcast.70, f32[2048,512]{0,1:T(8,128)S(1)} %copy-done.2, f32[2048]{0:T(1024)S(1)} %add_rsqrt_fusion, f32[2048]{0:T(1024)S(1)} %broadcast_multiply_fusion), kind=kOutput, calls=%fused_computation.60 | convolution fusion | flops 608698368 | bytes 6569984 | tf_op jit(solution)/shard_map/dot_general | solution.py:151
  (60 shorter events, 2.6 us)
Async XLA Ops:
  0.0 142.2 %copy-start = (bf16[512,256]{1,0:T(8,128)(2,1)S(1)}, bf16[512,256]{1,0:T(8,128)(2,1)}, u32[]{:S(2)}) copy-start(bf16[512,256]{1,0:T(8,128)(2,1)} %param.17) | copy-start | bytes 786436
  5.9 26.4 %copy-start.1 = (s32[32]{0:T(128)S(1)}, s32[32]{0:T(128)}, u32[]{:S(2)}) copy-start(s32[32]{0:T(128)} %param.11) | copy-start | bytes 388
  5.9 18.8 %all-to-all-start = ((bf16[4,2,256,256]{3,2,1,0:T(8,128)(2,1)}), bf16[4,2,256,256]{3,2,1,0:T(8,128)(2,1)S(1)}, u32[]{:S(2)}, u32[]{:S(2)}) async-start(bf16[4,2,256,256]{3,2,1,0:T(8,128)(2,1)} %broadcast_select_fusion.3), calls=%async_computation | async-start | bytes 2097152 | tf_op jit(solution)/shard_map/all_to_all | solution.py:98
  25.4 32.4 %copy-start.7 = (bf16[256,256]{1,0:T(8,128)(2,1)S(1)}, bf16[256,256]{1,0:T(8,128)(2,1)}, u32[]{:S(2)}) copy-start(bf16[256,256]{1,0:T(8,128)(2,1)} %param.13) | copy-start | bytes 393220
  26.5 31.0 %all-to-all-start.1 = ((bf16[4,2,256,256]{3,2,1,0:T(8,128)(2,1)}), bf16[4,2,256,256]{3,2,1,0:T(8,128)(2,1)S(1)}, u32[]{:S(2)}, u32[]{:S(2)}) async-start(bf16[4,2,256,256]{3,2,1,0:T(8,128)(2,1)} %bitcast.8), calls=%async_computation.1 | async-start | bytes 2097152 | tf_op jit(solution)/shard_map/all_to_all | solution.py:103
  58.9 1.5 copy-start.8
  82.0 4.9 %copy-start.6 = (s32[4,4,2]{1,2,0:T(2,128)S(1)}, s32[4,4,2]{1,2,0:T(2,128)}, u32[]{:S(2)}) copy-start(s32[4,4,2]{1,2,0:T(2,128)} %param.12) | copy-start | bytes 388
  83.2 28.8 %all-to-all-start.2 = ((bf16[4,1,2,256,256]{3,4,2,1,0:T(8,128)(2,1)}), bf16[4,1,2,256,256]{3,4,2,1,0:T(8,128)(2,1)S(1)}, u32[]{:S(2)}, u32[]{:S(2)}) async-start(bf16[4,1,2,256,256]{3,4,2,1,0:T(8,128)(2,1)} %pad_maximum_fusion.1), calls=%async_computation.2 | async-start | bytes 2097152 | tf_op jit(solution)/shard_map/all_to_all | solution.py:111
  112.7 5.9 %copy-start.3 = (bf16[8,256,256]{2,1,0:T(8,128)(2,1)S(1)}, bf16[8,256,256]{2,1,0:T(8,128)(2,1)}, u32[]{:S(2)}) copy-start(bf16[8,256,256]{2,1,0:T(8,128)(2,1)} %param.10) | copy-start | bytes 3145732
  113.3 5.3 %copy-start.4 = (bf16[512,512]{1,0:T(8,128)(2,1)S(1)}, bf16[512,512]{1,0:T(8,128)(2,1)}, u32[]{:S(2)}) copy-start(bf16[512,512]{1,0:T(8,128)(2,1)} %param.16) | copy-start | bytes 1572868
  114.6 17.9 %all-to-all-start.3 = ((bf16[4,2,256,256]{3,2,1,0:T(8,128)(2,1)}), bf16[4,2,256,256]{3,2,1,0:T(8,128)(2,1)S(1)}, u32[]{:S(2)}, u32[]{:S(2)}) async-start(bf16[4,2,256,256]{3,2,1,0:T(8,128)(2,1)} %broadcast_select_fusion.4), calls=%async_computation.3 | async-start | bytes 2097152 | tf_op jit(solution)/shard_map/all_to_all | solution.py:128
  133.1 0.9 copy-start.5
  139.4 3.4 %copy-start.2 = (f32[2048,512]{0,1:T(8,128)S(1)}, f32[2048,512]{0,1:T(8,128)}, u32[]{:S(2)}) copy-start(f32[2048,512]{0,1:T(8,128)} %get-tuple-element.45) | copy-start | bytes 12582916
